TPU v7x, 256 devices: a whole 4x4x8 slice. The times are simulated.
256 devices in a mesh: dp: 8 (over x, y_lo), cent: 16 (over z, y_hi), rep: 2 (over core).
Axes of the slice: x: 4, y: 4 (y_hi: 2, y_lo: 2; y = y_hi * 2 + y_lo), z: 8, core: 2. Of those that a mesh axis runs over, the one named last changes fastest.
Arguments:
- rows: bfloat16 [32768, 1024], P(('dp', 'rep')), may hold values from -15 to 15
- panel: bfloat16 [16384, 1024], P('cent'), may hold values from -2.15 to 2.15
- scales: float32 [16384, 8], P('cent'), may hold values from 0.7 to 1.4
- inv_temp: int32 [1], replicated, may hold values from 4 to 15
Outputs:
- centroid_sums: float32 [1024, 16384], P(('dp', 'rep'), 'cent')
- centroid_counts: float32 [16384], P('cent')
All inputs are finite; a program needn't handle non-finite values.
Results may differ from a plain program's by a relative error of at most 0.04.
Values may be sent and summed in bfloat16 or wider, within the bound.
No kernel may reach another device: no remote copies, remote signals or barrier semaphores. Data moves between devices by JAX's collectives and lax.ppermute only.
A program may use at most 64 MiB of HBM per device.

v0:
```python
import math

import jax
import jax.numpy as jnp
from jax import lax
from jax.sharding import PartitionSpec as P


def dequantize(panel, scales):
    count, width = panel.shape
    blocks = scales.shape[1]
    full = panel.astype(jnp.float32).reshape(count, blocks, width // blocks) * scales[:, :, None]
    return full.reshape(count, width).astype(jnp.bfloat16)


def stats_cent(local_max, local_total):
    top = lax.pmax(local_max, "cent")
    total = lax.psum(local_total * jnp.exp(local_max - top), "cent")
    return (top, total)


def local_logits(row_block, centroids, factor):
    norms = jnp.sum(centroids.astype(jnp.float32) ** 2, axis=1)
    prod = lax.dot_general(
        row_block, centroids, (((1,), (1,)), ((), ())), preferred_element_type=jnp.float32
    )
    return (prod - 0.5 * norms[None, :]) * factor


def on_device(rows, panel, scales, inv_temp):
    width = rows.shape[1]
    factor = inv_temp[0].astype(jnp.float32) / math.sqrt(width)
    centroids = dequantize(panel, scales)
    logits = local_logits(rows, centroids, factor)
    local_max = jnp.max(logits, axis=1)
    local_total = jnp.sum(jnp.exp(logits - local_max[:, None]), axis=1)
    top, total = stats_cent(local_max, local_total)
    weights = (jnp.exp(logits - top[:, None]) / total[:, None]).astype(jnp.bfloat16)
    sums = lax.psum_scatter(
        lax.dot_general(
            rows, weights, (((0,), (0,)), ((), ())), preferred_element_type=jnp.float32
        ),
        ("dp", "rep"),
        scatter_dimension=0,
        tiled=True,
    )
    counts = lax.psum(jnp.sum(weights.astype(jnp.float32), axis=0), ("dp", "rep"))
    return (sums, counts)


def solution(mesh):
    in_specs = (P(("dp", "rep"), None), P("cent", None), P("cent", None), P())
    out_specs = (P(("dp", "rep"), "cent"), P("cent"))
    return jax.shard_map(
        on_device, mesh=mesh, in_specs=in_specs, out_specs=out_specs, check_vma=False
    )
```

profile of v0, /device:TPU:32, one launch (start us, length us, event | category | flops | bytes accessed | tf_op | source)
XLA Modules:
  0.0 198.1 jit_solution(8743640233885203853)
XLA Ops:
  7.2 0.0 copy-start
  7.2 0.0 reduce-scatter.4.cloned.1.call-start
  8.0 1.0 copy.8
  9.0 1.1 mul.32
  10.1 0.0 copy-start.1
  10.1 0.0 copy-done
  10.1 0.7 multiply_reduce_fusion
  10.9 1.4 copy-done.1
  12.3 6.9 %fusion = (f32[2048]{0:T(1024)S(1)}, f32[1024,2048]{1,0:T(8,128)}) fusion(f32[]{:T(128)} %bitcast, f32[1024]{0:T(1024)S(1)} %broadcast_multiply_fusion, bf16[2048,1024]{1,0:T(8,128)(2,1)S(1)} %copy-done.1, f32[128,8,8,128]{3,2,1,0:T(8,128)S(1)} %bitcast.18, bf16[1024,1024]{1,0:T(8,128)(2,1)S(1)} %copy-done), kind=kOutput, calls=%fused_computation.4 | convolution fusion | flops 4304402432 | bytes 18886660 | tf_op jit(solution)/shard_map/dot_general | solution.py:24
  19.2 43.1 %pmax.7 = f32[2048]{0:T(1024)S(1)} all-reduce(f32[2048]{0:T(1024)S(1)} %get-tuple-element.8), channel_id=1, replica_groups=mesh['dp'=8,'cent'=16,'rep'=2] {'cent'}, use_global_device_ids=true, to_apply=%region_2.0 | all-reduce | flops 2048 | bytes 16384 | tf_op jit(solution)/shard_map/pmax | solution.py:17
  62.3 4.5 %exponential_reduce_fusion = f32[2048]{0:T(1024)S(1)} fusion(f32[1024,2048]{1,0:T(8,128)} %get-tuple-element.9, f32[2048]{0:T(1024)S(1)} %get-tuple-element.8, f32[]{:T(128)} %bitcast, f32[1024]{0:T(1024)S(1)} %broadcast_multiply_fusion), kind=kLoop, calls=%fused_computation.2 | loop fusion | flops 8386560 | bytes 8409092 | tf_op jit(solution)/shard_map/reduce_sum | solution.py:36
  66.8 37.1 %psum.14 = f32[2048]{0:T(1024)S(1)} all-reduce(f32[2048]{0:T(1024)S(1)} %exponential_multiply_fusion), channel_id=1, replica_groups=mesh['dp'=8,'cent'=16,'rep'=2] {'cent'}, use_global_device_ids=true, to_apply=%region_4.0 | all-reduce | flops 2048 | bytes 16384 | tf_op jit(solution)/shard_map/psum | solution.py:18
  104.0 0.0 copy-start.2
  104.0 4.9 %convert_reduce_fusion = (f32[1024]{0:T(1024)S(1)}, bf16[1024,2048]{1,0:T(8,128)(2,1)S(1)}) fusion(f32[2048]{0:T(1024)S(1)} %psum.14, f32[2048]{0:T(1024)S(1)} %pmax.7, f32[]{:T(128)} %bitcast, f32[1024,2048]{1,0:T(8,128)} %get-tuple-element.9, f32[1024]{0:T(1024)S(1)} %broadcast_multiply_fusion), kind=kLoop, calls=%fused_computation | loop fusion | flops 14679040 | bytes 12607492 | tf_op jit(solution)/shard_map/reduce_sum | solution.py:47
  108.8 0.0 copy-done.2
  108.8 6.0 %convolution_bitcast_fusion = f32[1024,1024]{0,1:T(8,128)} fusion(bf16[1024,2048]{1,0:T(8,128)(2,1)S(1)} %get-tuple-element.7, bf16[2048,1024]{1,0:T(8,128)(2,1)S(1)} %copy-done.2), kind=kOutput, calls=%fused_computation.8 | convolution fusion | flops 4294967296 | bytes 12582912 | tf_op jit(solution)/shard_map/dot_general | solution.py:40
  114.9 5.3 %copy.10 = f32[1024,1024]{1,0:T(8,128)} copy(f32[1024,1024]{0,1:T(8,128)} %convolution_bitcast_fusion) | data formatting | bytes 8388608
  120.2 0.0 reduce-scatter.4.cloned.1.call-update
  120.3 27.9 %psum.15 = f32[1024]{0:T(1024)} all-reduce(f32[1024]{0:T(1024)S(1)} %get-tuple-element.6), channel_id=1, replica_groups=mesh['dp'=8,'cent'=16,'rep'=2] {'dp','rep'}, use_global_device_ids=true, to_apply=%region_7.0 | all-reduce | flops 1024 | bytes 8192 | tf_op jit(solution)/shard_map/psum | solution.py:47
  148.2 43.1 %reduce-scatter.4.cloned.1.call-done = f32[64,1024]{1,0:T(8,128)} async-done(((f32[1024,1024]{1,0:T(8,128)}), f32[64,1024]{1,0:T(8,128)}) %reduce-scatter.4.cloned.1.call-update) | async-done | bytes 262160
  (2 shorter events, 0.0 us)
Async XLA Ops:
  7.2 3.0 %copy-start = (bf16[1024,1024]{1,0:T(8,128)(2,1)S(1)}, bf16[1024,1024]{1,0:T(8,128)(2,1)}, u32[]{:S(2)}) copy-start(bf16[1024,1024]{1,0:T(8,128)(2,1)} %param.5) | copy-start | bytes 6291460
  7.2 184.1 %reduce-scatter.4.cloned.1.call-start = ((), (), s32[]{:S(2)}) async-start(), calls=%async_computation.1 | async-start | bytes 4456448
  10.1 2.2 %copy-start.1 = (bf16[2048,1024]{1,0:T(8,128)(2,1)S(1)}, bf16[2048,1024]{1,0:T(8,128)(2,1)}, u32[]{:S(2)}) copy-start(bf16[2048,1024]{1,0:T(8,128)(2,1)} %param.4) | copy-start | bytes 12582916
  104.0 4.9 %copy-start.2 = (bf16[2048,1024]{1,0:T(8,128)(2,1)S(1)}, bf16[2048,1024]{1,0:T(8,128)(2,1)}, u32[]{:S(2)}) copy-start(bf16[2048,1024]{1,0:T(8,128)(2,1)} %param.4) | copy-start | bytes 12582916
Sparse Core Ops, SparseCore 0:
  120.4 70.8 reduce-scatter.3
where the time goes:
time: 198 us
  blocking collectives  108 us (55%)
  waiting for transfers between devices  43.1 us (22%)
  between operations  14.9 us (8%)
  matrix products  12.9 us (7%)
  other arithmetic  10.1 us (5%)
  local copies, waits for them, and re-layouts  8.86 us (4%)
    unnamed x2, waiting for transfers between devices  43.1 us
    pmax x1, blocking collectives, stats_cent(): top = lax.pmax(local_max, 'cent')  43.1 us
    psum x1, blocking collectives, stats_cent(): total = lax.psum(local_total * jnp.exp(local_max - top), 'cent')  37.1 us
    psum x1, blocking collectives, on_device(): lax.psum(jnp.sum(weights.astype(jnp.float32), axis=0), ('dp', 'rep'))  27.9 us
    unnamed x8, local copies, waits for them, and re-layouts  7.72 us
    dot_general x1, matrix products, local_logits(): lax.dot_general(row_block, centroids, (((1,), (1,)), ((), ())), preferred...  6.88 us
    dot_general x1, matrix products, on_device(): lax.dot_general(rows, weights, (((0,), (0,)), ((), ())), preferred_elemen...  6.05 us
    reduce_sum x1, other arithmetic, on_device(): jnp.sum(weights.astype(jnp.float32), axis=0)  4.85 us
  transfers between devices with their start and end apart: 1, of which 1 were waited for; matrix products, arithmetic and copies ran while one was open for 0% of the time, Pallas kernels for 0%

commit v1 on v0

v1 whole, which is shorter than its diff:
```python
import math

import jax
import jax.numpy as jnp
from jax import lax
from jax.experimental import pallas as pl
from jax.experimental.pallas import tpu as pltpu
from jax.sharding import PartitionSpec as P

BLOCK = 128
COLS = ((0, 384), (384, 768), (768, 1024))
RB = 256
EXTRA = 8
NT = (((1,), (1,)), ((), ()))
VMEM = pl.BlockSpec(memory_space=pltpu.VMEM)
SMEM = pl.BlockSpec(memory_space=pltpu.SMEM)
ANY = pl.BlockSpec(memory_space=pl.ANY)
PARAMS = pltpu.CompilerParams(vmem_limit_bytes=56 * 1024 * 1024)


def assign_kernel(
    fac_ref, scales_ref, panel_hbm, rows_hbm, expo_ref, stat_ref,
    panel, rows, cent, half, la, lb, psem, rsem,
):
    count, width = panel.shape
    total = rows.shape[0]
    kb = count // 4
    nrow = total // RB

    def pcopy(i):
        part = pl.ds(i * kb, kb)
        return pltpu.make_async_copy(panel_hbm.at[part], panel.at[part], psem.at[i])

    def rcopy(i):
        part = pl.ds(i * RB, RB)
        return pltpu.make_async_copy(rows_hbm.at[part], rows.at[part], rsem.at[i])

    for i in range(4):
        pcopy(i).start()
    for i in range(nrow):
        rcopy(i).start()
    cols = jnp.transpose(scales_ref[...])
    for i in range(4):
        pcopy(i).wait()
        norm = jnp.zeros((kb, BLOCK), jnp.float32)
        for b in range(width // BLOCK):
            x = panel[i * kb:(i + 1) * kb, b * BLOCK:(b + 1) * BLOCK].astype(jnp.float32)
            c = (x * cols[i * kb:(i + 1) * kb, b:b + 1]).astype(jnp.bfloat16)
            cent[i * kb:(i + 1) * kb, b * BLOCK:(b + 1) * BLOCK] = c
            c = c.astype(jnp.float32)
            norm = norm + c * c
        norm = 0.5 * jnp.sum(norm, axis=1, keepdims=True)
        half[i * kb:(i + 1) * kb, :] = jnp.broadcast_to(norm, (kb, BLOCK))
    fac = fac_ref[0]

    def product(i, out):
        part = pl.ds(pl.multiple_of(i * RB, RB), RB)
        out[...] = lax.dot_general(cent[...], rows[part, :], NT, preferred_element_type=jnp.float32)

    def soft(i, buf):
        tops, sums = [], []
        for t in range(RB // BLOCK):
            lanes = pl.ds(t * BLOCK, BLOCK)
            logits = (buf[:, lanes] - half[...]) * fac
            top = jnp.max(logits, axis=0, keepdims=True)
            expo = jnp.exp2(logits - top)
            out = pl.ds(pl.multiple_of(i * RB + t * BLOCK, BLOCK), BLOCK)
            expo_ref[:, out] = expo.astype(jnp.bfloat16)
            stat_ref[0:1, out] = top
            stat_ref[1:2, out] = top + jnp.log2(jnp.sum(expo, axis=0, keepdims=True))

    rcopy(0).wait()
    product(0, la)

    def pair(j, carry):
        i = 2 * j
        rcopy(i + 1).wait()
        product(i + 1, lb)
        soft(i, la)
        rcopy(i + 2).wait()
        product(i + 2, la)
        soft(i + 1, lb)
        return carry

    lax.fori_loop(0, nrow // 2 - 1, pair, 0)
    rcopy(nrow - 1).wait()
    product(nrow - 1, lb)
    soft(nrow - 2, la)
    soft(nrow - 1, lb)


def assign(rows, panel, scales_t, fac):
    total, width = rows.shape
    count = panel.shape[0]
    return pl.pallas_call(
        assign_kernel,
        out_shape=(
            jax.ShapeDtypeStruct((count, total), jnp.bfloat16),
            jax.ShapeDtypeStruct((2, total), jnp.float32),
        ),
        in_specs=[SMEM, VMEM, ANY, ANY],
        out_specs=(VMEM, VMEM),
        scratch_shapes=[
            pltpu.VMEM((count, width), jnp.bfloat16),
            pltpu.VMEM((total, width), jnp.bfloat16),
            pltpu.VMEM((count, width), jnp.bfloat16),
            pltpu.VMEM((count, BLOCK), jnp.float32),
            pltpu.VMEM((count, RB), jnp.float32),
            pltpu.VMEM((count, RB), jnp.float32),
            pltpu.SemaphoreType.DMA((4,)),
            pltpu.SemaphoreType.DMA((total // RB,)),
        ],
        compiler_params=PARAMS,
        cost_estimate=pl.CostEstimate(
            flops=2 * total * width * count, bytes_accessed=10 * 1024 * 1024, transcendentals=total * count
        ),
        name="assign",
    )(fac, scales_t, panel, rows)


def flip_kernel(place_ref, rows_ref, out_ref):
    total, width = rows_ref.shape
    for t in range(width // 128):
        turned = jnp.transpose(rows_ref[:, t * 128:(t + 1) * 128])
        for r in range(2):
            at = pl.multiple_of(place_ref[2 * t + r], 64)
            out_ref[pl.ds(at, 64), :] = turned[r * 64:(r + 1) * 64, :]
    out_ref[width:, :] = jnp.ones((EXTRA, total), jnp.bfloat16)


def flip(rows, place):
    total, width = rows.shape
    return pl.pallas_call(
        flip_kernel,
        out_shape=jax.ShapeDtypeStruct((width + EXTRA, total), jnp.bfloat16),
        in_specs=[SMEM, VMEM],
        out_specs=VMEM,
        compiler_params=PARAMS,
        cost_estimate=pl.CostEstimate(flops=0, bytes_accessed=8 * 1024 * 1024, transcendentals=0),
        name="flip",
    )(place, rows)


def order(j):
    spots = []
    for p in range(8):
        bits = [(p >> 2) & 1, (p >> 1) & 1, p & 1]
        bits = bits[j:] + bits[:j]
        spots.append(bits[0] * 4 + bits[1] * 2 + bits[2])
    return spots


def counted(block):
    hi = block.astype(jnp.bfloat16).astype(jnp.float32)
    row = lax.broadcasted_iota(jnp.int32, block.shape, 0)
    return jnp.where(row % 2 == 0, hi, block - hi)


def rounded(block):
    hi = block.astype(jnp.bfloat16).astype(jnp.float32)
    return hi + (block - hi).astype(jnp.bfloat16).astype(jnp.float32)


def sums_kernel(stat_ref, lse_ref, lhs_ref, expo_ref, send_ref, keep_ref):
    width = lhs_ref.shape[0] - EXTRA
    half = width // 2
    scale = jnp.exp2(stat_ref[0:1, :] - lse_ref[...])
    for j, (a, b) in enumerate(COLS):
        w = (expo_ref[a:b, :].astype(jnp.float32) * scale).astype(jnp.bfloat16)
        acc = lax.dot_general(lhs_ref[...], w, NT, preferred_element_type=jnp.float32)
        for p, q in enumerate(order(j)):
            keep_ref[q * 64:(q + 1) * 64, a:b] = acc[p * 64:(p + 1) * 64, :]
            send_ref[q * 64:(q + 1) * 64, a:b] = acc[half + p * 64:half + (p + 1) * 64, :].astype(jnp.bfloat16)
        keep_ref[half:, a:b] = acc[width:, :]
        send_ref[half:, a:b] = counted(acc[width:, :]).astype(jnp.bfloat16)


def weighted(stat, lse, lhs, expo):
    half = (lhs.shape[0] - EXTRA) // 2
    count = expo.shape[0]
    return pl.pallas_call(
        sums_kernel,
        out_shape=(
            jax.ShapeDtypeStruct((half + EXTRA, count), jnp.bfloat16),
            jax.ShapeDtypeStruct((half + EXTRA, count), jnp.float32),
        ),
        in_specs=[VMEM] * 4,
        out_specs=(VMEM, VMEM),
        compiler_params=PARAMS,
        cost_estimate=pl.CostEstimate(
            flops=2 * lhs.shape[0] * lhs.shape[1] * count, bytes_accessed=12 * 1024 * 1024, transcendentals=2048
        ),
        name="sums",
    )(stat, lse, lhs, expo)


def added(keep, recv):
    h = keep.shape[0] - EXTRA
    total = keep[:h, :] + recv[:h, :].astype(jnp.float32)
    got = recv[h:, :].astype(jnp.float32)
    other = got[0:1, :] + got[1:2, :]
    return total, rounded(keep[h:, :]) + other


def fold(keeps, recvs):
    n = len(keeps)
    h = (keeps[0].shape[0] - EXTRA) // 2

    def kernel(*refs):
        for j in range(n):
            total, count = added(refs[j], refs[n + j])
            send, keep = refs[2 * n + 2 * j], refs[2 * n + 2 * j + 1]
            keep[:h, :] = total[:h, :]
            keep[h:, :] = count
            send[:h, :] = total[h:, :].astype(jnp.bfloat16)
            send[h:, :] = counted(count).astype(jnp.bfloat16)

    shapes = []
    for k in keeps:
        shapes += [
            jax.ShapeDtypeStruct((h + EXTRA, k.shape[1]), jnp.bfloat16),
            jax.ShapeDtypeStruct((h + EXTRA, k.shape[1]), jnp.float32),
        ]
    out = pl.pallas_call(
        kernel, out_shape=shapes, in_specs=[VMEM] * (2 * n), out_specs=[VMEM] * (2 * n),
        compiler_params=PARAMS, name="fold",
    )(*keeps, *recvs)
    return out[0::2], out[1::2]


def split(keep, recv):
    n = len(COLS)
    h = (keep.shape[0] - EXTRA) // 2

    def kernel(keep_ref, recv_ref, *outs):
        for j, (a, b) in enumerate(COLS):
            total, count = added(keep_ref[:, a:b], recv_ref[:, a:b])
            outs[2 * j + 1][:h, :] = total[:h, :]
            outs[2 * j + 1][h:, :] = count
            outs[2 * j][:h, :] = total[h:, :].astype(jnp.bfloat16)
            outs[2 * j][h:, :] = counted(count).astype(jnp.bfloat16)

    shapes = []
    for a, b in COLS:
        shapes += [
            jax.ShapeDtypeStruct((h + EXTRA, b - a), jnp.bfloat16),
            jax.ShapeDtypeStruct((h + EXTRA, b - a), jnp.float32),
        ]
    out = pl.pallas_call(
        kernel, out_shape=shapes, in_specs=[VMEM] * 2, out_specs=[VMEM] * (2 * n),
        compiler_params=PARAMS, name="split",
    )(keep, recv)
    return out[0::2], out[1::2]


def finish(keeps, recvs):
    n = len(keeps)
    h = keeps[0].shape[0] - EXTRA
    count = COLS[-1][1]

    def kernel(*refs):
        for j, (a, b) in enumerate(COLS):
            total, cnt = added(refs[j], refs[n + j])
            refs[2 * n][:, a:b] = total
            refs[2 * n + 1][:, a:b] = cnt[0:1, :]

    return pl.pallas_call(
        kernel,
        out_shape=(jax.ShapeDtypeStruct((h, count), jnp.float32), jax.ShapeDtypeStruct((1, count), jnp.float32)),
        in_specs=[VMEM] * (2 * n), out_specs=(VMEM, VMEM), compiler_params=PARAMS, name="finish",
    )(*keeps, *recvs)


def joined(parts):
    top = parts[0]
    for p in parts[1:]:
        top = jnp.maximum(top, p)
    total = jnp.exp2(parts[0] - top)
    for p in parts[1:]:
        total = total + jnp.exp2(p - top)
    return top + jnp.log2(total)


def cent_move(x, dz, dh):
    pairs = [(z * 2 + h, ((z + dz) % 8) * 2 + (h ^ dh)) for z in range(8) for h in range(2)]
    return lax.ppermute(x, "cent", pairs)


def flipped(x, axis, n, mask):
    return lax.ppermute(x, axis, [(i, i ^ mask) for i in range(n)])


def on_device(rows, panel, scales, inv_temp):
    width = rows.shape[1]
    fac = inv_temp.astype(jnp.float32) * (math.log2(math.e) / math.sqrt(width))
    expo, stat = assign(rows, panel, scales.T, fac)

    dp, rep = lax.axis_index("dp"), lax.axis_index("rep")
    x, y = dp // 2, dp % 2
    code = y * 4 + jnp.where((x == 1) | (x == 2), 2, 0) + jnp.where(x >= 2, 1, 0)
    place = []
    for t in range(8):
        tx, ty = t // 2, t % 2
        theirs = ty * 4 + (2 if tx in (1, 2) else 0) + (1 if tx >= 2 else 0)
        spot = (code ^ theirs) * 64
        place += [spot + 512 * rep, spot + 512 * (1 - rep)]
    place = jnp.stack(place).astype(jnp.int32)
    lhs = flip(rows, place)

    lse = stat[1:2]
    lse = joined([lse, cent_move(lse, 1, 0), cent_move(lse, -1, 0), cent_move(lse, 0, 1)])
    lse = joined([lse, cent_move(lse, 4, 0), cent_move(lse, 2, 1), cent_move(lse, -2, 1)])

    send, keep = weighted(stat, lse, lhs, expo)
    sends, keeps = split(keep, flipped(send, "rep", 2, 1))
    masks = (1, 2, 6)
    for s in range(3):
        recvs = [flipped(c, "dp", 8, masks[(j + s) % 3]) for j, c in enumerate(sends)]
        if s < 2:
            sends, keeps = fold(keeps, recvs)
    sums, counts = finish(keeps, recvs)
    return (sums, counts[0])


def solution(mesh):
    in_specs = (P(("dp", "rep"), None), P("cent", None), P("cent", None), P())
    out_specs = (P(("dp", "rep"), "cent"), P("cent"))
    return jax.shard_map(
        on_device, mesh=mesh, in_specs=in_specs, out_specs=out_specs, check_vma=False
    )
```

time: 198 us -> 94.8 us (0.48)
  blocking collectives: 108 us -> 0 us
  Pallas kernels: 0 us -> 41.5 us
  starting transfers between devices: 0.04 us -> 25.1 us
  waiting for transfers between devices: 43.1 us -> 20.1 us
  between operations: 14.9 us -> 1.36 us
  matrix products: 12.9 us -> 0 us
  other arithmetic: 10.1 us -> 1.46 us
  local copies, waits for them, and re-layouts: 8.86 us -> 4.49 us
    psum x2 -> x0, blocking collectives: 65.1 us -> none  [the longest x1 37.1 us: stats_cent(): total = lax.psum(local_total * jnp.exp(local_max - top), 'cent')]
    unnamed x2 -> x0, waiting for transfers between devices: 43.1 us -> none
    pmax x1 -> x0, blocking collectives: 43.1 us -> none  [stats_cent(): top = lax.pmax(local_max, 'cent')]
    pallas_call x0 -> x7, Pallas kernels: none -> 41.5 us  [the longest x1 16.1 us: assign(): pl.pallas_call(assign_kernel, out_shape=(jax.ShapeDtypeStruct((count, tot...]
    ppermute x0 -> x16, starting transfers between devices: none -> 25.1 us  [the longest x6 14.1 us: cent_move(): return lax.ppermute(x, 'cent', pairs)]
    ppermute x0 -> x16, waiting for transfers between devices: none -> 20.1 us  [the longest x10 14.6 us: flipped(): return lax.ppermute(x, axis, [(i, i ^ mask) for i in range(n)])]
    dot_general x2 -> x0, matrix products: 12.9 us -> none  [the longest x1 6.88 us: local_logits(): lax.dot_general(row_block, centroids, (((1,), (1,)), ((), ())), preferred...]
    reduce_sum x3 -> x0, other arithmetic: 10.1 us -> none  [the longest x1 4.85 us: on_device(): jnp.sum(weights.astype(jnp.float32), axis=0)]
  transfers between devices with their start and end apart: 1 -> 16, of which waited for: 1 -> 6; matrix products, arithmetic and copies ran while one was open for 0% -> 1% of each run, Pallas kernels for 0% -> 6%
where the time goes in v1:
time: 94.8 us; the launch traced here: 94 us
  Pallas kernels  41.5 us (44%)
  starting transfers between devices  25.1 us (26%)
  waiting for transfers between devices  20.1 us (21%)
  local copies, waits for them, and re-layouts  4.49 us (5%)
  other arithmetic  1.46 us (2%)
  between operations  1.36 us (1%)
    pallas_call x1, Pallas kernels, assign(): pl.pallas_call(assign_kernel, out_shape=(jax.ShapeDtypeStruct((count, tot...  16.1 us
    ppermute x10, waiting for transfers between devices, flipped(): return lax.ppermute(x, axis, [(i, i ^ mask) for i in range(n)])  14.6 us
    ppermute x6, starting transfers between devices, cent_move(): return lax.ppermute(x, 'cent', pairs)  14.1 us
    ppermute x10, starting transfers between devices, flipped(): return lax.ppermute(x, axis, [(i, i ^ mask) for i in range(n)])  11 us
    pallas_call x1, Pallas kernels, weighted(): pl.pallas_call(sums_kernel, out_shape=(jax.ShapeDtypeStruct((half + EXTRA...  10.9 us
    ppermute x6, waiting for transfers between devices, cent_move(): return lax.ppermute(x, 'cent', pairs)  5.57 us
    pallas_call x1, Pallas kernels, flip(): pl.pallas_call(flip_kernel, out_shape=jax.ShapeDtypeStruct((width + EXTRA...  5.4 us
    pallas_call x2, Pallas kernels, fold(): pl.pallas_call(kernel, out_shape=shapes, in_specs=[VMEM] * (2 * n), out_s...  4.32 us
  transfers between devices with their start and end apart: 16, of which 6 were waited for; matrix products, arithmetic and copies ran while one was open for 1% of the time, Pallas kernels for 6%

profile of v1, /device:TPU:32, one launch (start us, length us, event | category | flops | bytes accessed | tf_op | source)
XLA Modules:
  0.0 94.0 jit_solution(13731275198197983998)
XLA Ops:
  1.3 16.1 %assign.1 = (bf16[1024,2048]{1,0:T(8,128)(2,1)}, f32[2,2048]{1,0:T(2,128)}) custom-call(f32[1]{0:T(128)S(6)} %mul.24.fac_ref, f32[8,1024]{1,0:T(8,128)} %bitcast.18, bf16[1024,1024]{1,0:T(8,128)(2,1)} %panel_hbm.1, bf16[2048,1024]{1,0:T(8,128)(2,1)} %rows_ref.1), custom_call_target="tpu_custom_call" | custom-call | flops 4294967296 | bytes 10485760 | tf_op jit(solution)/shard_map/assign/pallas_call | solution.py:95
  18.1 1.9 %collective-permute-start.1 = (f32[1,2048]{1,0:T(1,128)S(1)}, f32[1,2048]{1,0:T(1,128)S(1)}, u32[]{:S(2)}, u32[]{:S(2)}) collective-permute-start(f32[1,2048]{1,0:T(1,128)S(1)} %slice.3), channel_id=1, source_target_pairs={{0,28},{2,30},{4,0},{6,2},{8,4},{10,6},{12,8},{14,10},{16,12},{18,... | collective-permute-start | bytes 24584 | tf_op jit(solution)/shard_map/ppermute | solution.py:286
  20.0 1.5 %collective-permute-start.2 = (f32[1,2048]{1,0:T(1,128)S(1)}, f32[1,2048]{1,0:T(1,128)S(1)}, u32[]{:S(2)}, u32[]{:S(2)}) collective-permute-start(f32[1,2048]{1,0:T(1,128)S(1)} %slice.3), channel_id=1, source_target_pairs={{0,2},{2,0},{4,6},{6,4},{8,10},{10,8},{12,14},{14,12},{16,18},{18,... | collective-permute-start | bytes 24584 | tf_op jit(solution)/shard_map/ppermute | solution.py:286
  21.5 1.9 %collective-permute-start = (f32[1,2048]{1,0:T(1,128)S(1)}, f32[1,2048]{1,0:T(1,128)S(1)}, u32[]{:S(2)}, u32[]{:S(2)}) collective-permute-start(f32[1,2048]{1,0:T(1,128)S(1)} %slice.3), channel_id=1, source_target_pairs={{0,4},{2,6},{4,8},{6,10},{8,12},{10,14},{12,16},{14,18},{16,20},{1... | collective-permute-start | bytes 24584 | tf_op jit(solution)/shard_map/ppermute | solution.py:286
  23.4 1.8 %collective-permute-done.2 = f32[1,2048]{1,0:T(1,128)S(1)} collective-permute-done((f32[1,2048]{1,0:T(1,128)S(1)}, f32[1,2048]{1,0:T(1,128)S(1)}, u32[]{:S(2)}, u32[]{:S(2)}) %collective-permute-start.2) | collective-permute-done | bytes 8224 | tf_op jit(solution)/shard_map/ppermute | solution.py:286
  25.2 3.8 %collective-permute-done = f32[1,2048]{1,0:T(1,128)S(1)} collective-permute-done((f32[1,2048]{1,0:T(1,128)S(1)}, f32[1,2048]{1,0:T(1,128)S(1)}, u32[]{:S(2)}, u32[]{:S(2)}) %collective-permute-start) | collective-permute-done | bytes 8224 | tf_op jit(solution)/shard_map/ppermute | solution.py:286
  29.8 3.5 %collective-permute-start.5 = (f32[1,2048]{1,0:T(1,128)S(1)}, f32[1,2048]{1,0:T(1,128)S(1)}, u32[]{:S(2)}, u32[]{:S(2)}) collective-permute-start(f32[1,2048]{1,0:T(1,128)S(1)} %multiply_add_fusion.1), channel_id=1, source_target_pairs={{0,26},{2,24},{4,30},{6,28},{8,2},{10,0},{12,6},{14,4},{16,10},{18... | collective-permute-start | bytes 24584 | tf_op jit(solution)/shard_map/ppermute | solution.py:286
  33.3 1.9 %collective-permute-start.4 = (f32[1,2048]{1,0:T(1,128)S(1)}, f32[1,2048]{1,0:T(1,128)S(1)}, u32[]{:S(2)}, u32[]{:S(2)}) collective-permute-start(f32[1,2048]{1,0:T(1,128)S(1)} %multiply_add_fusion.1), channel_id=1, source_target_pairs={{0,10},{2,8},{4,14},{6,12},{8,18},{10,16},{12,22},{14,20},{16,26},... | collective-permute-start | bytes 24584 | tf_op jit(solution)/shard_map/ppermute | solution.py:286
  35.2 3.4 %collective-permute-start.3 = (f32[1,2048]{1,0:T(1,128)S(1)}, f32[1,2048]{1,0:T(1,128)S(1)}, u32[]{:S(2)}, u32[]{:S(2)}) collective-permute-start(f32[1,2048]{1,0:T(1,128)S(1)} %multiply_add_fusion.1), channel_id=1, source_target_pairs={{0,16},{2,18},{4,20},{6,22},{8,24},{10,26},{12,28},{14,30},{16,0},... | collective-permute-start | bytes 24584 | tf_op jit(solution)/shard_map/ppermute | solution.py:286
  39.2 5.4 %flip.1.lhs_ref = bf16[1032,2048]{1,0:T(8,128)(2,1)} custom-call(s32[16]{0:T(128)} %stack.67.place_ref, bf16[2048,1024]{1,0:T(8,128)(2,1)} %rows_ref.1), custom_call_target="tpu_custom_call" | custom-call | bytes 8388608 | tf_op jit(solution)/shard_map/flip/pallas_call | solution.py:133
  45.2 10.9 %sums.1 = (bf16[520,1024]{1,0:T(8,128)(2,1)}, f32[520,1024]{1,0:T(8,128)}) custom-call(f32[2,2048]{1,0:T(2,128)} %get-tuple-element.26.stat_ref, f32[1,2048]{1,0:T(1,128)} %multiply_add_fusion.lse_ref, bf16[1032,2048]{1,0:T(8,128)(2,1)} %flip.1.lhs_ref, bf16[1024,2048]{1,0:T(8,128)(2,1)} %get-tuple-element.27.expo_ref), custom_call_target="tpu_custom_call" | custom-call | flops 4328521728 | bytes 12582912 | tf_op jit(solution)/shard_map/sums/pallas_call | solution.py:181
  56.1 2.9 %collective-permute-done.6.recv_ref = bf16[520,1024]{1,0:T(8,128)(2,1)S(1)} collective-permute-done((bf16[520,1024]{1,0:T(8,128)(2,1)}, bf16[520,1024]{1,0:T(8,128)(2,1)S(1)}, u32[]{:S(2)}, u32[]{:S(2)}) %collective-permute-start.6) | collective-permute-done | bytes 1064992 | tf_op jit(solution)/shard_map/ppermute | solution.py:290
  60.0 3.0 %split.1 = (bf16[264,384]{1,0:T(8,128)(2,1)}, f32[264,384]{1,0:T(8,128)}, bf16[264,384]{1,0:T(8,128)(2,1)}, f32[264,384]{1,0:T(8,128)}, bf16[264,256]{1,0:T(8,128)(2,1)}, /*index=5*/f32[264,256]{1,0:T(8,128)}) custom-call(f32[520,1024]{1,0:T(8,128)} %get-tuple-element.28.keep_ref, bf16[520,1024]{1,0:T(8,128)(2,1)} %copy-done), custom_call_target="tpu_custom_call" | custom-call | tf_op jit(solution)/shard_map/split/pallas_call | solution.py:249
  63.7 1.5 %collective-permute-start.8 = (bf16[264,384]{1,0:T(8,128)(2,1)}, bf16[264,384]{1,0:T(8,128)(2,1)S(1)}, u32[]{:S(2)}, u32[]{:S(2)}) collective-permute-start(bf16[264,384]{1,0:T(8,128)(2,1)} %get-tuple-element.34), channel_id=1, source_target_pairs={{0,64},{32,96},{64,0},{96,32},{128,192},{160,224},{192,128},{224,1... | collective-permute-start | bytes 608264 | tf_op jit(solution)/shard_map/ppermute | solution.py:290
  65.2 2.1 %collective-permute-start.9 = (bf16[264,256]{1,0:T(8,128)(2,1)}, bf16[264,256]{1,0:T(8,128)(2,1)S(1)}, u32[]{:S(2)}, u32[]{:S(2)}) collective-permute-start(bf16[264,256]{1,0:T(8,128)(2,1)} %get-tuple-element.35), channel_id=1, source_target_pairs={{0,192},{32,224},{64,128},{96,160},{128,64},{160,96},{192,0},{224,... | collective-permute-start | bytes 405512 | tf_op jit(solution)/shard_map/ppermute | solution.py:290
  67.3 4.4 %collective-permute-done.9.refs_5_ = bf16[264,256]{1,0:T(8,128)(2,1)S(1)} collective-permute-done((bf16[264,256]{1,0:T(8,128)(2,1)}, bf16[264,256]{1,0:T(8,128)(2,1)S(1)}, u32[]{:S(2)}, u32[]{:S(2)}) %collective-permute-start.9) | collective-permute-done | bytes 135200 | tf_op jit(solution)/shard_map/ppermute | solution.py:290
  72.5 2.3 %fold.2 = (bf16[136,384]{1,0:T(8,128)(2,1)}, f32[136,384]{1,0:T(8,128)}, bf16[136,384]{1,0:T(8,128)(2,1)}, f32[136,384]{1,0:T(8,128)}, bf16[136,256]{1,0:T(8,128)(2,1)}, /*index=5*/f32[136,256]{1,0:T(8,128)}) custom-call(f32[264,384]{1,0:T(8,128)} %get-tuple-element.30.refs_0_, f32[264,384]{1,0:T(8,128)} %get-tuple-element.31.refs_1_, ...), custom_call_target="tpu_custom_call" | custom-call | tf_op jit(solution)/shard_map/fold/pallas_call | solution.py:224
  75.2 2.1 %collective-permute-start.11 = (bf16[136,384]{1,0:T(8,128)(2,1)}, bf16[136,384]{1,0:T(8,128)(2,1)S(1)}, u32[]{:S(2)}, u32[]{:S(2)}) collective-permute-start(bf16[136,384]{1,0:T(8,128)(2,1)} %get-tuple-element.40), channel_id=1, source_target_pairs={{0,192},{32,224},{64,128},{96,160},{128,64},{160,96},{192,0},{224,... | collective-permute-start | bytes 313352 | tf_op jit(solution)/shard_map/ppermute | solution.py:290
  77.3 1.3 %collective-permute-start.12 = (bf16[136,256]{1,0:T(8,128)(2,1)}, bf16[136,256]{1,0:T(8,128)(2,1)S(1)}, u32[]{:S(2)}, u32[]{:S(2)}) collective-permute-start(bf16[136,256]{1,0:T(8,128)(2,1)} %get-tuple-element.41), channel_id=1, source_target_pairs={{0,32},{32,0},{64,96},{96,64},{128,160},{160,128},{192,224},{224,1... | collective-permute-start | bytes 208904 | tf_op jit(solution)/shard_map/ppermute | solution.py:290
  78.7 3.2 %collective-permute-done.12.refs_5_ = bf16[136,256]{1,0:T(8,128)(2,1)S(1)} collective-permute-done((bf16[136,256]{1,0:T(8,128)(2,1)}, bf16[136,256]{1,0:T(8,128)(2,1)S(1)}, u32[]{:S(2)}, u32[]{:S(2)}) %collective-permute-start.12) | collective-permute-done | bytes 69664 | tf_op jit(solution)/shard_map/ppermute | solution.py:290
  82.6 2.0 %fold.3 = (bf16[72,384]{1,0:T(8,128)(2,1)}, f32[72,384]{1,0:T(8,128)}, bf16[72,384]{1,0:T(8,128)(2,1)}, f32[72,384]{1,0:T(8,128)}, bf16[72,256]{1,0:T(8,128)(2,1)}, /*index=5*/f32[72,256]{1,0:T(8,128)}) custom-call(f32[136,384]{1,0:T(8,128)} %get-tuple-element.36.refs_0_, f32[136,384]{1,0:T(8,128)} %get-tuple-element.37.refs_1_, ...), custom_call_target="tpu_custom_call" | custom-call | tf_op jit(solution)/shard_map/fold/pallas_call | solution.py:224
  84.6 1.5 %collective-permute-start.13 = (bf16[72,384]{1,0:T(8,128)(2,1)}, bf16[72,384]{1,0:T(8,128)(2,1)S(1)}, u32[]{:S(2)}, u32[]{:S(2)}) collective-permute-start(bf16[72,384]{1,0:T(8,128)(2,1)} %get-tuple-element.45), channel_id=1, source_target_pairs={{0,192},{32,224},{64,128},{96,160},{128,64},{160,96},{192,0},{224,... | collective-permute-start | bytes 165896 | tf_op jit(solution)/shard_map/ppermute | solution.py:290
  87.5 4.1 %collective-permute-done.15.refs_5_ = bf16[72,256]{1,0:T(8,128)(2,1)S(1)} collective-permute-done((bf16[72,256]{1,0:T(8,128)(2,1)}, bf16[72,256]{1,0:T(8,128)(2,1)S(1)}, u32[]{:S(2)}, u32[]{:S(2)}) %collective-permute-start.15) | collective-permute-done | bytes 36896 | tf_op jit(solution)/shard_map/ppermute | solution.py:290
  92.3 1.8 %finish.1 = (f32[64,1024]{1,0:T(8,128)}, f32[1,1024]{1,0:T(1,128)}) custom-call(f32[72,384]{1,0:T(8,128)} %get-tuple-element.42.refs_0_, f32[72,384]{1,0:T(8,128)} %get-tuple-element.43.refs_1_, f32[72,256]{1,0:T(8,128)} %get-tuple-element.44.refs_2_, bf16[72,384]{1,0:T(8,128)(2,1)} %copy-done.7, bf16[72,384]{1,0:T(8,128)(2,1)} %copy-done.8, ...), custom_call_target="tpu_custom_call" | custom-call | tf_op jit(solution)/shard_map/finish/pallas_call | solution.py:267
  (39 shorter events, 8.5 us)
Async XLA Ops:
  18.1 5.3 %collective-permute-start.1 = (f32[1,2048]{1,0:T(1,128)S(1)}, f32[1,2048]{1,0:T(1,128)S(1)}, u32[]{:S(2)}, u32[]{:S(2)}) collective-permute-start(f32[1,2048]{1,0:T(1,128)S(1)} %slice.3), channel_id=1, source_target_pairs={{0,28},{2,30},{4,0},{6,2},{8,4},{10,6},{12,8},{14,10},{16,12},{18,... | collective-permute-start | bytes 24584 | tf_op jit(solution)/shard_map/ppermute | solution.py:286
  20.0 5.2 %collective-permute-start.2 = (f32[1,2048]{1,0:T(1,128)S(1)}, f32[1,2048]{1,0:T(1,128)S(1)}, u32[]{:S(2)}, u32[]{:S(2)}) collective-permute-start(f32[1,2048]{1,0:T(1,128)S(1)} %slice.3), channel_id=1, source_target_pairs={{0,2},{2,0},{4,6},{6,4},{8,10},{10,8},{12,14},{14,12},{16,18},{18,... | collective-permute-start | bytes 24584 | tf_op jit(solution)/shard_map/ppermute | solution.py:286
  21.5 7.5 %collective-permute-start = (f32[1,2048]{1,0:T(1,128)S(1)}, f32[1,2048]{1,0:T(1,128)S(1)}, u32[]{:S(2)}, u32[]{:S(2)}) collective-permute-start(f32[1,2048]{1,0:T(1,128)S(1)} %slice.3), channel_id=1, source_target_pairs={{0,4},{2,6},{4,8},{6,10},{8,12},{10,14},{12,16},{14,18},{16,20},{1... | collective-permute-start | bytes 24584 | tf_op jit(solution)/shard_map/ppermute | solution.py:286
  29.8 14.8 %collective-permute-start.5 = (f32[1,2048]{1,0:T(1,128)S(1)}, f32[1,2048]{1,0:T(1,128)S(1)}, u32[]{:S(2)}, u32[]{:S(2)}) collective-permute-start(f32[1,2048]{1,0:T(1,128)S(1)} %multiply_add_fusion.1), channel_id=1, source_target_pairs={{0,26},{2,24},{4,30},{6,28},{8,2},{10,0},{12,6},{14,4},{16,10},{18... | collective-permute-start | bytes 24584 | tf_op jit(solution)/shard_map/ppermute | solution.py:286
  33.3 11.3 %collective-permute-start.4 = (f32[1,2048]{1,0:T(1,128)S(1)}, f32[1,2048]{1,0:T(1,128)S(1)}, u32[]{:S(2)}, u32[]{:S(2)}) collective-permute-start(f32[1,2048]{1,0:T(1,128)S(1)} %multiply_add_fusion.1), channel_id=1, source_target_pairs={{0,10},{2,8},{4,14},{6,12},{8,18},{10,16},{12,22},{14,20},{16,26},... | collective-permute-start | bytes 24584 | tf_op jit(solution)/shard_map/ppermute | solution.py:286
  35.2 9.4 %collective-permute-start.3 = (f32[1,2048]{1,0:T(1,128)S(1)}, f32[1,2048]{1,0:T(1,128)S(1)}, u32[]{:S(2)}, u32[]{:S(2)}) collective-permute-start(f32[1,2048]{1,0:T(1,128)S(1)} %multiply_add_fusion.1), channel_id=1, source_target_pairs={{0,16},{2,18},{4,20},{6,22},{8,24},{10,26},{12,28},{14,30},{16,0},... | collective-permute-start | bytes 24584 | tf_op jit(solution)/shard_map/ppermute | solution.py:286
  56.1 2.9 %collective-permute-start.6 = (bf16[520,1024]{1,0:T(8,128)(2,1)}, bf16[520,1024]{1,0:T(8,128)(2,1)S(1)}, u32[]{:S(2)}, u32[]{:S(2)}) collective-permute-start(bf16[520,1024]{1,0:T(8,128)(2,1)} %get-tuple-element.29), channel_id=1, source_target_pairs={{0,1},{1,0},{2,3},{3,2},{4,5},{5,4},{6,7},{7,6},{8,9},{9,8},{10,11... | collective-permute-start | bytes 3194888 | tf_op jit(solution)/shard_map/ppermute | solution.py:290
  59.0 1.0 %copy-start = (bf16[520,1024]{1,0:T(8,128)(2,1)}, bf16[520,1024]{1,0:T(8,128)(2,1)S(1)}, u32[]{:S(2)}) copy-start(bf16[520,1024]{1,0:T(8,128)(2,1)S(1)} %collective-permute-done.6.recv_ref) | copy-start | bytes 3194884
  63.0 8.7 %collective-permute-start.7 = (bf16[264,384]{1,0:T(8,128)(2,1)}, bf16[264,384]{1,0:T(8,128)(2,1)S(1)}, u32[]{:S(2)}, u32[]{:S(2)}) collective-permute-start(bf16[264,384]{1,0:T(8,128)(2,1)} %get-tuple-element.33), channel_id=1, source_target_pairs={{0,32},{32,0},{64,96},{96,64},{128,160},{160,128},{192,224},{224,1... | collective-permute-start | bytes 608264 | tf_op jit(solution)/shard_map/ppermute | solution.py:290
  63.7 8.0 %collective-permute-start.8 = (bf16[264,384]{1,0:T(8,128)(2,1)}, bf16[264,384]{1,0:T(8,128)(2,1)S(1)}, u32[]{:S(2)}, u32[]{:S(2)}) collective-permute-start(bf16[264,384]{1,0:T(8,128)(2,1)} %get-tuple-element.34), channel_id=1, source_target_pairs={{0,64},{32,96},{64,0},{96,32},{128,192},{160,224},{192,128},{224,1... | collective-permute-start | bytes 608264 | tf_op jit(solution)/shard_map/ppermute | solution.py:290
  65.2 6.5 %collective-permute-start.9 = (bf16[264,256]{1,0:T(8,128)(2,1)}, bf16[264,256]{1,0:T(8,128)(2,1)S(1)}, u32[]{:S(2)}, u32[]{:S(2)}) collective-permute-start(bf16[264,256]{1,0:T(8,128)(2,1)} %get-tuple-element.35), channel_id=1, source_target_pairs={{0,192},{32,224},{64,128},{96,160},{128,64},{160,96},{192,0},{224,... | collective-permute-start | bytes 405512 | tf_op jit(solution)/shard_map/ppermute | solution.py:290
  71.7 0.6 copy-start.3
  71.7 0.7 copy-start.1
  71.7 0.8 copy-start.2
  74.8 7.0 %collective-permute-start.10 = (bf16[136,384]{1,0:T(8,128)(2,1)}, bf16[136,384]{1,0:T(8,128)(2,1)S(1)}, u32[]{:S(2)}, u32[]{:S(2)}) collective-permute-start(bf16[136,384]{1,0:T(8,128)(2,1)} %get-tuple-element.39), channel_id=1, source_target_pairs={{0,64},{32,96},{64,0},{96,32},{128,192},{160,224},{192,128},{224,1... | collective-permute-start | bytes 313352 | tf_op jit(solution)/shard_map/ppermute | solution.py:290
  75.2 6.6 %collective-permute-start.11 = (bf16[136,384]{1,0:T(8,128)(2,1)}, bf16[136,384]{1,0:T(8,128)(2,1)S(1)}, u32[]{:S(2)}, u32[]{:S(2)}) collective-permute-start(bf16[136,384]{1,0:T(8,128)(2,1)} %get-tuple-element.40), channel_id=1, source_target_pairs={{0,192},{32,224},{64,128},{96,160},{128,64},{160,96},{192,0},{224,... | collective-permute-start | bytes 313352 | tf_op jit(solution)/shard_map/ppermute | solution.py:290
  77.3 4.5 %collective-permute-start.12 = (bf16[136,256]{1,0:T(8,128)(2,1)}, bf16[136,256]{1,0:T(8,128)(2,1)S(1)}, u32[]{:S(2)}, u32[]{:S(2)}) collective-permute-start(bf16[136,256]{1,0:T(8,128)(2,1)} %get-tuple-element.41), channel_id=1, source_target_pairs={{0,32},{32,0},{64,96},{96,64},{128,160},{160,128},{192,224},{224,1... | collective-permute-start | bytes 208904 | tf_op jit(solution)/shard_map/ppermute | solution.py:290
  81.8 0.7 copy-start.4
  81.8 0.7 copy-start.5
  84.6 7.0 %collective-permute-start.13 = (bf16[72,384]{1,0:T(8,128)(2,1)}, bf16[72,384]{1,0:T(8,128)(2,1)S(1)}, u32[]{:S(2)}, u32[]{:S(2)}) collective-permute-start(bf16[72,384]{1,0:T(8,128)(2,1)} %get-tuple-element.45), channel_id=1, source_target_pairs={{0,192},{32,224},{64,128},{96,160},{128,64},{160,96},{192,0},{224,... | collective-permute-start | bytes 165896 | tf_op jit(solution)/shard_map/ppermute | solution.py:290
  86.1 5.5 %collective-permute-start.14 = (bf16[72,384]{1,0:T(8,128)(2,1)}, bf16[72,384]{1,0:T(8,128)(2,1)S(1)}, u32[]{:S(2)}, u32[]{:S(2)}) collective-permute-start(bf16[72,384]{1,0:T(8,128)(2,1)} %get-tuple-element.46), channel_id=1, source_target_pairs={{0,32},{32,0},{64,96},{96,64},{128,160},{160,128},{192,224},{224,1... | collective-permute-start | bytes 165896 | tf_op jit(solution)/shard_map/ppermute | solution.py:290
  87.4 4.2 %collective-permute-start.15 = (bf16[72,256]{1,0:T(8,128)(2,1)}, bf16[72,256]{1,0:T(8,128)(2,1)S(1)}, u32[]{:S(2)}, u32[]{:S(2)}) collective-permute-start(bf16[72,256]{1,0:T(8,128)(2,1)} %get-tuple-element.47), channel_id=1, source_target_pairs={{0,64},{32,96},{64,0},{96,32},{128,192},{160,224},{192,128},{224,1... | collective-permute-start | bytes 110600 | tf_op jit(solution)/shard_map/ppermute | solution.py:290
  91.6 0.6 copy-start.7
  91.6 0.7 copy-start.8
  (2 other events, 1.2 us)

commit v2 on v0

v2 whole, which is shorter than its diff:
```python
import math

import jax
import jax.numpy as jnp
from jax import lax
from jax.experimental import pallas as pl
from jax.experimental.pallas import tpu as pltpu
from jax.sharding import PartitionSpec as P

BLOCK = 128
RB = 512
KB = 256
SB = 128
SPLIT = 2
EXTRA = 8
PARTS = 2
NT = (((1,), (1,)), ((), ()))
VMEM = pl.BlockSpec(memory_space=pltpu.VMEM)
SMEM = pl.BlockSpec(memory_space=pltpu.SMEM)
HBM = pl.BlockSpec(memory_space=pltpu.HBM)


def limit(mib):
    return pltpu.CompilerParams(vmem_limit_bytes=mib * 1024 * 1024)


def assign_kernel(
    fac_ref, scales_ref, panel_hbm, rows_hbm, expo_ref, top_ref, lse_ref,
    panel, rows, cent, half, psem, rsem,
):
    count, width = panel.shape
    total = rows.shape[0]
    nk, nr = count // KB, total // RB

    def pcopy(i):
        part = pl.ds(i * KB, KB)
        return pltpu.make_async_copy(panel_hbm.at[part], panel.at[part], psem.at[i])

    def rcopy(i):
        part = pl.ds(i * RB, RB)
        return pltpu.make_async_copy(rows_hbm.at[part], rows.at[part], rsem.at[i])

    pcopy(0).start()
    pcopy(1).start()
    rcopy(0).start()
    for i in range(2, nk):
        pcopy(i).start()
    for i in range(1, nr):
        rcopy(i).start()
    cols = jnp.transpose(scales_ref[...])
    fac = fac_ref[0]

    def dequantize(i):
        ks = slice(i * KB, (i + 1) * KB)
        norm = None
        for b in range(width // BLOCK):
            ds = slice(b * BLOCK, (b + 1) * BLOCK)
            c = (panel[ks, ds].astype(jnp.float32) * cols[ks, b:b + 1]).astype(jnp.bfloat16)
            cent[ks, ds] = c
            c = c.astype(jnp.float32)
            norm = c * c if norm is None else norm + c * c
        norm = 0.5 * jnp.sum(norm, axis=1, keepdims=True)
        half[ks, :] = jnp.broadcast_to(norm, (KB, BLOCK))

    def product(i, first, size):
        ks = slice(first, first + size)
        at = slice(i * RB, (i + 1) * RB)
        expo_ref[ks, at] = lax.dot_general(
            cent[ks, :], rows[at, :], NT, preferred_element_type=jnp.float32
        )

    def soft(i, t):
        at = slice(i * RB + t * BLOCK, i * RB + (t + 1) * BLOCK)
        top = jnp.full((8, BLOCK), -jnp.inf, jnp.float32)
        for g in range(0, count, SB):
            ks = slice(g, g + SB)
            dist = (expo_ref[ks, at] - half[ks, :]).reshape(SB // 8, 8, BLOCK)
            top = jnp.maximum(top, jnp.max(dist, axis=0))
        top = jnp.max(top, axis=0, keepdims=True)
        tot = jnp.zeros((8, BLOCK), jnp.float32)
        for g in range(0, count, SB):
            ks = slice(g, g + SB)
            expo = jnp.exp2(((expo_ref[ks, at] - half[ks, :]) - top) * fac)
            expo_ref[ks, at] = expo
            tot = tot + jnp.sum(expo.reshape(SB // 8, 8, BLOCK), axis=0)
        top = top * fac
        top_ref[:, at] = top
        lse_ref[:, at] = top + jnp.log2(jnp.sum(tot, axis=0, keepdims=True))

    pcopy(0).wait()
    dequantize(0)
    for i in range(1, nk):
        pcopy(i).wait()
    rcopy(0).wait()
    for i in range(nk):
        product(0, i * KB, KB)
        if i + 1 < nk:
            dequantize(i + 1)
    for i in range(1, nr):
        rcopy(i).wait()
    tiles = RB // BLOCK
    for i in range(1, nr):
        for j in range(SPLIT):
            product(i, j * count // SPLIT, count // SPLIT)
            for t in range(j * tiles // SPLIT, (j + 1) * tiles // SPLIT):
                soft(i - 1, t)
    for t in range(tiles):
        soft(nr - 1, t)


def assign(rows, panel, scales_t, fac):
    total, width = rows.shape
    count = panel.shape[0]
    line = jax.ShapeDtypeStruct((1, total), jnp.float32)
    return pl.pallas_call(
        assign_kernel,
        out_shape=(jax.ShapeDtypeStruct((count, total), jnp.float32), line, line),
        in_specs=[SMEM, VMEM, HBM, HBM],
        out_specs=(VMEM, VMEM, VMEM),
        scratch_shapes=[
            pltpu.VMEM((count, width), jnp.bfloat16),
            pltpu.VMEM((total, width), jnp.bfloat16),
            pltpu.VMEM((count, width), jnp.bfloat16),
            pltpu.VMEM((count, BLOCK), jnp.float32),
            pltpu.SemaphoreType.DMA((count // KB,)),
            pltpu.SemaphoreType.DMA((total // RB,)),
        ],
        compiler_params=limit(24),
        cost_estimate=pl.CostEstimate(
            flops=2 * total * width * count, bytes_accessed=10 * 1024 * 1024, transcendentals=total * count
        ),
        name="assign",
    )(fac, scales_t, *(pltpu.with_memory_space_constraint(x, pltpu.HBM) for x in (panel, rows)))


def bits_of(x, y):
    one, two = x % 2, x // 2
    return y, one + two - 2 * one * two, two


def flip_kernel(rows_ref, out_ref):
    total, width = rows_ref.shape
    dp, rep = lax.axis_index("dp"), lax.axis_index("rep")
    mine = bits_of(dp // 2, dp % 2)
    for t in range(width // 128):
        turned = jnp.transpose(rows_ref[:, t * 128:(t + 1) * 128])
        y, a, b = [m + o - 2 * m * o for m, o in zip(mine, bits_of(t // 2, t % 2))]
        for r, spot in enumerate((4 * y + 2 * a + b, 4 * a + 2 * b + y)):
            other = rep + r - 2 * rep * r
            at = pl.multiple_of(spot * 64 + other * (width // 2), 64)
            out_ref[pl.ds(at, 64), :] = turned[r * 64:(r + 1) * 64, :]
    out_ref[width:, :] = jnp.ones((EXTRA, total), jnp.bfloat16)


def flip(rows, part):
    total, width = rows.shape
    total = total // 2
    return pl.pallas_call(
        flip_kernel,
        grid=(1,),
        out_shape=jax.ShapeDtypeStruct((width + EXTRA, total), jnp.bfloat16),
        in_specs=[pl.BlockSpec((total, width), lambda i: (part, 0))],
        out_specs=VMEM,
        compiler_params=limit(14),
        cost_estimate=pl.CostEstimate(flops=0, bytes_accessed=4 * 1024 * 1024, transcendentals=0),
        name="flip",
    )(rows)


def join(parts):
    def kernel(*refs):
        vals = [r[...] for r in refs[:-1]]
        top = vals[0]
        for v in vals[1:]:
            top = jnp.maximum(top, v)
        total = jnp.exp2(vals[0] - top)
        for v in vals[1:]:
            total = total + jnp.exp2(v - top)
        refs[-1][...] = top + jnp.log2(total)

    return pl.pallas_call(
        kernel, out_shape=jax.ShapeDtypeStruct(parts[0].shape, jnp.float32),
        in_specs=[VMEM] * len(parts), out_specs=VMEM, compiler_params=limit(2), name="join",
    )(*parts)


def counted(block):
    hi = block.astype(jnp.bfloat16).astype(jnp.float32)
    row = lax.broadcasted_iota(jnp.int32, block.shape, 0)
    return jnp.where(row % 2 == 0, hi, block - hi).astype(jnp.bfloat16)


def rounded(block):
    hi = block.astype(jnp.bfloat16).astype(jnp.float32)
    return hi + (block - hi).astype(jnp.bfloat16).astype(jnp.float32)


def sums_kernel(part, top_ref, lse_ref, lhs0_ref, lhs1_ref, expo_ref, send_ref, keep_ref):
    width = lhs0_ref.shape[0] - EXTRA
    half = width // 2
    cols = send_ref.shape[1]
    scale = jnp.exp2(top_ref[...] - lse_ref[...])
    acc = None
    n = lhs0_ref.shape[1]
    for j, lhs in enumerate((lhs0_ref, lhs1_ref)):
        ex = expo_ref[part * cols:(part + 1) * cols, j * n:(j + 1) * n]
        w = (ex * scale[:, j * n:(j + 1) * n]).astype(jnp.bfloat16)
        one = lax.dot_general(lhs[...], w, NT, preferred_element_type=jnp.float32)
        acc = one if acc is None else acc + one
    keep_ref[:half, :] = acc[:half, :]
    keep_ref[half:, :] = acc[width:, :]
    send_ref[:half, :] = acc[half:width, :].astype(jnp.bfloat16)
    send_ref[half:, :] = counted(acc[width:, :])


def weighted(part, top, lse, lhs0, lhs1, expo):
    half = (lhs0.shape[0] - EXTRA) // 2
    cols = expo.shape[0] // PARTS

    def kernel(*refs):
        sums_kernel(part, *refs)

    return pl.pallas_call(
        kernel,
        out_shape=(
            jax.ShapeDtypeStruct((half + EXTRA, cols), jnp.bfloat16),
            jax.ShapeDtypeStruct((half + EXTRA, cols), jnp.float32),
        ),
        in_specs=[VMEM] * 5,
        out_specs=(VMEM, VMEM),
        compiler_params=limit(16),
        cost_estimate=pl.CostEstimate(
            flops=2 * lhs0.shape[0] * expo.shape[1] * cols, bytes_accessed=1024 * 1024, transcendentals=2048
        ),
        name="sums",
    )(top, lse, lhs0, lhs1, expo)


def added(keep, recv):
    h = keep.shape[0] - EXTRA
    total = keep[:h, :] + recv[:h, :].astype(jnp.float32)
    got = recv[h:, :].astype(jnp.float32)
    return total, rounded(keep[h:, :]) + (got[0:1, :] + got[1:2, :])


def fold(keep, recv):
    h = (keep.shape[0] - EXTRA) // 2

    def kernel(keep_ref, recv_ref, send_ref, next_ref):
        total, count = added(keep_ref, recv_ref)
        next_ref[:h, :] = total[:h, :]
        next_ref[h:, :] = count
        send_ref[:h, :] = total[h:, :].astype(jnp.bfloat16)
        send_ref[h:, :] = counted(count)

    shape = (h + EXTRA, keep.shape[1])
    return pl.pallas_call(
        kernel,
        out_shape=(jax.ShapeDtypeStruct(shape, jnp.bfloat16), jax.ShapeDtypeStruct(shape, jnp.float32)),
        in_specs=[VMEM] * 2, out_specs=(VMEM, VMEM), compiler_params=limit(4), name="fold",
    )(keep, recv)


def finish(keeps, recvs):
    n = len(keeps)
    h = keeps[0].shape[0] - EXTRA
    cols = keeps[0].shape[1]

    def kernel(*refs):
        for j in range(n):
            total, count = added(refs[j], refs[n + j])
            refs[2 * n][:, j * cols:(j + 1) * cols] = total
            refs[2 * n + 1][:, j * cols:(j + 1) * cols] = count[0:1, :]

    return pl.pallas_call(
        kernel,
        out_shape=(
            jax.ShapeDtypeStruct((h, n * cols), jnp.float32),
            jax.ShapeDtypeStruct((1, n * cols), jnp.float32),
        ),
        in_specs=[VMEM] * (2 * n), out_specs=(VMEM, VMEM), compiler_params=limit(4), name="finish",
    )(*keeps, *recvs)


def cent_move(x, dz, dh):
    pairs = [(z * 2 + h, ((z + dz) % 8) * 2 + (h ^ dh)) for z in range(8) for h in range(2)]
    return lax.ppermute(x, "cent", pairs)


def swap(x):
    return lax.ppermute(x, "rep", [(0, 1), (1, 0)])


def exchange(x, step):
    masks = ((1, 2, 6), (2, 6, 1))
    pairs = [(d * 2 + r, (d ^ masks[r][step]) * 2 + r) for d in range(8) for r in range(2)]
    return lax.ppermute(x, ("dp", "rep"), pairs)


def on_device(rows, panel, scales, inv_temp):
    width = rows.shape[1]
    fac = inv_temp.astype(jnp.float32) * (math.log2(math.e) / math.sqrt(width))
    expo, top, lse = assign(rows, panel, scales.T, fac)
    lhs0 = flip(rows, 0)
    lhs1 = flip(rows, 1)

    lse = join([lse, cent_move(lse, 1, 0), cent_move(lse, -1, 0), cent_move(lse, 0, 1)])
    lse = join([lse, cent_move(lse, 4, 0), cent_move(lse, 2, 1), cent_move(lse, -2, 1)])

    pairs = [weighted(j, top, lse, lhs0, lhs1, expo) for j in range(PARTS)]
    sends, keeps = [p[0] for p in pairs], [p[1] for p in pairs]
    recvs = [swap(s) for s in sends]
    for step in range(3):
        pairs = [fold(k, r) for k, r in zip(keeps, recvs)]
        sends, keeps = [p[0] for p in pairs], [p[1] for p in pairs]
        recvs = [exchange(s, step) for s in sends]
    sums, counts = finish(keeps, recvs)
    return (sums, counts[0])


def solution(mesh):
    in_specs = (P(("dp", "rep"), None), P("cent", None), P("cent", None), P())
    out_specs = (P(("dp", "rep"), "cent"), P("cent"))
    return jax.shard_map(
        on_device, mesh=mesh, in_specs=in_specs, out_specs=out_specs, check_vma=False
    )
```

time: 198 us -> 64.3 us (0.32)
  blocking collectives: 108 us -> 0 us
  starting transfers between devices: 0.04 us -> 29.3 us
  waiting for transfers between devices: 43.1 us -> 14.8 us
  Pallas kernels: 0 us -> 17 us
  between operations: 14.9 us -> 1.38 us
  matrix products: 12.9 us -> 0 us
  other arithmetic: 10.1 us -> 0 us
  local copies, waits for them, and re-layouts: 8.86 us -> 0.75 us
    psum x2 -> x0, blocking collectives: 65.1 us -> none  [the longest x1 37.1 us: stats_cent(): total = lax.psum(local_total * jnp.exp(local_max - top), 'cent')]
    unnamed x2 -> x0, waiting for transfers between devices: 43.1 us -> none
    pmax x1 -> x0, blocking collectives: 43.1 us -> none  [stats_cent(): top = lax.pmax(local_max, 'cent')]
    ppermute x0 -> x14, starting transfers between devices: none -> 29.3 us  [the longest x6 18.2 us: cent_move(): return lax.ppermute(x, 'cent', pairs)]
    pallas_call x0 -> x14, Pallas kernels: none -> 17 us  [the longest x1 9.73 us: assign(): pl.pallas_call(assign_kernel, out_shape=(jax.ShapeDtypeStruct((count, tot...]
    ppermute x0 -> x14, waiting for transfers between devices: none -> 14.8 us  [the longest x6 8.93 us: exchange(): return lax.ppermute(x, ('dp', 'rep'), pairs)]
    dot_general x2 -> x0, matrix products: 12.9 us -> none  [the longest x1 6.88 us: local_logits(): lax.dot_general(row_block, centroids, (((1,), (1,)), ((), ())), preferred...]
    reduce_sum x3 -> x0, other arithmetic: 10.1 us -> none  [the longest x1 4.85 us: on_device(): jnp.sum(weights.astype(jnp.float32), axis=0)]
  transfers between devices with their start and end apart: 1 -> 14, of which waited for: 1 -> 9; matrix products, arithmetic and copies ran while one was open for 0% -> 0% of each run, Pallas kernels for 0% -> 6%
where the time goes in v2:
time: 64.3 us; the launch traced here: 63.2 us
  starting transfers between devices  29.3 us (46%)
  Pallas kernels  17 us (26%)
  waiting for transfers between devices  14.8 us (23%)
  between operations  1.38 us (2%)
  local copies, waits for them, and re-layouts  0.75 us (1%)
    ppermute x6, starting transfers between devices, cent_move(): return lax.ppermute(x, 'cent', pairs)  18.2 us
    ppermute x6, starting transfers between devices, exchange(): return lax.ppermute(x, ('dp', 'rep'), pairs)  10.4 us
    pallas_call x1, Pallas kernels, assign(): pl.pallas_call(assign_kernel, out_shape=(jax.ShapeDtypeStruct((count, tot...  9.73 us
    ppermute x6, waiting for transfers between devices, exchange(): return lax.ppermute(x, ('dp', 'rep'), pairs)  8.93 us
    ppermute x6, waiting for transfers between devices, cent_move(): return lax.ppermute(x, 'cent', pairs)  5.23 us
    pallas_call x2, Pallas kernels, weighted(): pl.pallas_call(kernel, out_shape=(jax.ShapeDtypeStruct((half + EXTRA, col...  4.86 us
  transfers between devices with their start and end apart: 14, of which 9 were waited for; matrix products, arithmetic and copies ran while one was open for 0% of the time, Pallas kernels for 6%

profile of v2, /device:TPU:32, one launch (start us, length us, event | category | flops | bytes accessed | tf_op | source)
XLA Modules:
  0.0 63.2 jit_solution(3645479073102691366)
XLA Ops:
  1.3 0.7 %copy-done.1 = f32[1024,8]{0,1:T(8,128)S(1)} copy-done((f32[1024,8]{0,1:T(8,128)S(1)}, f32[1024,8]{0,1:T(8,128)}, u32[]{:S(2)}) %copy-start.1) | copy-done | bytes 32792
  2.0 9.7 %assign.1 = (f32[1024,2048]{1,0:T(8,128)S(1)}, f32[1,2048]{1,0:T(1,128)S(1)}, f32[1,2048]{1,0:T(1,128)S(1)}) custom-call(f32[1]{0:T(128)S(6)} %mul.3.fac_ref, f32[8,1024]{1,0:T(8,128)S(1)} %bitcast.2, bf16[1024,1024]{1,0:T(8,128)(2,1)} %panel_hbm.1, bf16[2048,1024]{1,0:T(8,128)(2,1)} %rows_ref.3), custom_call_target="tpu_custom_call" | custom-call | flops 4294967296 | bytes 10485760 | tf_op jit(solution)/shard_map/assign/pallas_call | solution.py:115
  11.8 2.0 %collective-permute-start = (f32[1,2048]{1,0:T(1,128)S(1)}, f32[1,2048]{1,0:T(1,128)S(1)}, u32[]{:S(2)}, u32[]{:S(2)}) collective-permute-start(f32[1,2048]{1,0:T(1,128)S(1)} %get-tuple-element.24.refs_0_), channel_id=1, source_target_pairs={{0,4},{2,6},{4,8},{6,10},{8,12},{10,14},{12,16},{14,18},{16,20},{1... | collective-permute-start | bytes 24584 | tf_op jit(solution)/shard_map/ppermute | solution.py:287
  13.9 3.2 %collective-permute-start.2 = (f32[1,2048]{1,0:T(1,128)S(1)}, f32[1,2048]{1,0:T(1,128)S(1)}, u32[]{:S(2)}, u32[]{:S(2)}) collective-permute-start(f32[1,2048]{1,0:T(1,128)S(1)} %get-tuple-element.24.refs_0_), channel_id=1, source_target_pairs={{0,2},{2,0},{4,6},{6,4},{8,10},{10,8},{12,14},{14,12},{16,18},{18,... | collective-permute-start | bytes 24584 | tf_op jit(solution)/shard_map/ppermute | solution.py:287
  17.4 1.6 %collective-permute-done.2.refs_3_ = f32[1,2048]{1,0:T(1,128)S(1)} collective-permute-done((f32[1,2048]{1,0:T(1,128)S(1)}, f32[1,2048]{1,0:T(1,128)S(1)}, u32[]{:S(2)}, u32[]{:S(2)}) %collective-permute-start.2) | collective-permute-done | bytes 8224 | tf_op jit(solution)/shard_map/ppermute | solution.py:287
  19.1 6.4 %collective-permute-start.3 = (f32[1,2048]{1,0:T(1,128)S(1)}, f32[1,2048]{1,0:T(1,128)S(1)}, u32[]{:S(2)}, u32[]{:S(2)}) collective-permute-start(f32[1,2048]{1,0:T(1,128)S(1)} %join.2.refs_0_), channel_id=1, source_target_pairs={{0,16},{2,18},{4,20},{6,22},{8,24},{10,26},{12,28},{14,30},{16,0},... | collective-permute-start | bytes 24584 | tf_op jit(solution)/shard_map/ppermute | solution.py:287
  25.4 4.1 %collective-permute-start.4 = (f32[1,2048]{1,0:T(1,128)S(1)}, f32[1,2048]{1,0:T(1,128)S(1)}, u32[]{:S(2)}, u32[]{:S(2)}) collective-permute-start(f32[1,2048]{1,0:T(1,128)S(1)} %join.2.refs_0_), channel_id=1, source_target_pairs={{0,10},{2,8},{4,14},{6,12},{8,18},{10,16},{12,22},{14,20},{16,26},... | collective-permute-start | bytes 24584 | tf_op jit(solution)/shard_map/ppermute | solution.py:287
  29.5 2.4 %collective-permute-start.5 = (f32[1,2048]{1,0:T(1,128)S(1)}, f32[1,2048]{1,0:T(1,128)S(1)}, u32[]{:S(2)}, u32[]{:S(2)}) collective-permute-start(f32[1,2048]{1,0:T(1,128)S(1)} %join.2.refs_0_), channel_id=1, source_target_pairs={{0,26},{2,24},{4,30},{6,28},{8,2},{10,0},{12,6},{14,4},{16,10},{18... | collective-permute-start | bytes 24584 | tf_op jit(solution)/shard_map/ppermute | solution.py:287
  32.6 0.6 flip.3.refs_3_
  33.6 2.9 %collective-permute-done.5.refs_3_ = f32[1,2048]{1,0:T(1,128)S(1)} collective-permute-done((f32[1,2048]{1,0:T(1,128)S(1)}, f32[1,2048]{1,0:T(1,128)S(1)}, u32[]{:S(2)}, u32[]{:S(2)}) %collective-permute-start.5) | collective-permute-done | bytes 8224 | tf_op jit(solution)/shard_map/ppermute | solution.py:287
  36.5 2.4 %sums.3 = (bf16[520,512]{1,0:T(8,128)(2,1)S(1)}, f32[520,512]{1,0:T(8,128)S(1)}) custom-call(f32[1,2048]{1,0:T(1,128)S(1)} %get-tuple-element.23.refs_0_, f32[1,2048]{1,0:T(1,128)S(1)} %join.3.refs_1_, bf16[1032,1024]{1,0:T(8,128)(2,1)S(1)} %flip.2.refs_2_, bf16[1032,1024]{1,0:T(8,128)(2,1)S(1)} %flip.3.refs_3_, f32[1024,2048]{1,0:T(8,128)S(1)} %get-tuple-element.25.refs_4_), custom_call_target="tpu_custom_call" | custom-call | flops 2164260864 | bytes 1048576 | tf_op jit(solution)/shard_map/sums/pallas_call | solution.py:223
  39.0 2.4 %sums.2 = (bf16[520,512]{1,0:T(8,128)(2,1)S(1)}, f32[520,512]{1,0:T(8,128)S(1)}) custom-call(f32[1,2048]{1,0:T(1,128)S(1)} %get-tuple-element.23.refs_0_, f32[1,2048]{1,0:T(1,128)S(1)} %join.3.refs_1_, bf16[1032,1024]{1,0:T(8,128)(2,1)S(1)} %flip.2.refs_2_, bf16[1032,1024]{1,0:T(8,128)(2,1)S(1)} %flip.3.refs_3_, f32[1024,2048]{1,0:T(8,128)S(1)} %get-tuple-element.25.refs_4_), custom_call_target="tpu_custom_call" | custom-call | flops 2164260864 | bytes 1048576 | tf_op jit(solution)/shard_map/sums/pallas_call | solution.py:223
  42.2 0.8 %collective-permute-start.10 = (bf16[264,512]{1,0:T(8,128)(2,1)S(1)}, bf16[264,512]{1,0:T(8,128)(2,1)S(1)}, u32[]{:S(2)}, u32[]{:S(2)}) collective-permute-start(bf16[264,512]{1,0:T(8,128)(2,1)S(1)} %get-tuple-element.36), channel_id=1, source_target_pairs={{0,32},{1,65},{32,0},{33,97},{64,96},{65,1},{96,64},{97,33},{128,1... | collective-permute-start | bytes 811016 | tf_op jit(solution)/shard_map/ppermute | solution.py:297
  42.9 0.7 %collective-permute-done.6.recv_ref = bf16[520,512]{1,0:T(8,128)(2,1)S(1)} collective-permute-done((bf16[520,512]{1,0:T(8,128)(2,1)S(1)}, bf16[520,512]{1,0:T(8,128)(2,1)S(1)}, u32[]{:S(2)}, u32[]{:S(2)}) %collective-permute-start.6) | collective-permute-done | bytes 532512 | tf_op jit(solution)/shard_map/ppermute | solution.py:291
  43.7 0.8 %collective-permute-start.7 = (bf16[264,512]{1,0:T(8,128)(2,1)S(1)}, bf16[264,512]{1,0:T(8,128)(2,1)S(1)}, u32[]{:S(2)}, u32[]{:S(2)}) collective-permute-start(bf16[264,512]{1,0:T(8,128)(2,1)S(1)} %get-tuple-element.29), channel_id=1, source_target_pairs={{0,32},{1,65},{32,0},{33,97},{64,96},{65,1},{96,64},{97,33},{128,1... | collective-permute-start | bytes 811016 | tf_op jit(solution)/shard_map/ppermute | solution.py:297
  44.5 4.2 %collective-permute-done.10.recv_ref = bf16[264,512]{1,0:T(8,128)(2,1)S(1)} collective-permute-done((bf16[264,512]{1,0:T(8,128)(2,1)S(1)}, bf16[264,512]{1,0:T(8,128)(2,1)S(1)}, u32[]{:S(2)}, u32[]{:S(2)}) %collective-permute-start.10) | collective-permute-done | bytes 270368 | tf_op jit(solution)/shard_map/ppermute | solution.py:297
  48.8 1.6 %collective-permute-start.11 = (bf16[136,512]{1,0:T(8,128)(2,1)S(1)}, bf16[136,512]{1,0:T(8,128)(2,1)S(1)}, u32[]{:S(2)}, u32[]{:S(2)}) collective-permute-start(bf16[136,512]{1,0:T(8,128)(2,1)S(1)} %get-tuple-element.38), channel_id=1, source_target_pairs={{0,64},{1,193},{32,96},{33,225},{64,0},{65,129},{96,32},{97,161},{... | collective-permute-start | bytes 417800 | tf_op jit(solution)/shard_map/ppermute | solution.py:297
  50.4 1.3 %collective-permute-done.7.recv_ref = bf16[264,512]{1,0:T(8,128)(2,1)S(1)} collective-permute-done((bf16[264,512]{1,0:T(8,128)(2,1)S(1)}, bf16[264,512]{1,0:T(8,128)(2,1)S(1)}, u32[]{:S(2)}, u32[]{:S(2)}) %collective-permute-start.7) | collective-permute-done | bytes 270368 | tf_op jit(solution)/shard_map/ppermute | solution.py:297
  51.7 1.6 %collective-permute-start.8 = (bf16[136,512]{1,0:T(8,128)(2,1)S(1)}, bf16[136,512]{1,0:T(8,128)(2,1)S(1)}, u32[]{:S(2)}, u32[]{:S(2)}) collective-permute-start(bf16[136,512]{1,0:T(8,128)(2,1)S(1)} %get-tuple-element.31), channel_id=1, source_target_pairs={{0,64},{1,193},{32,96},{33,225},{64,0},{65,129},{96,32},{97,161},{... | collective-permute-start | bytes 417800 | tf_op jit(solution)/shard_map/ppermute | solution.py:297
  53.3 0.7 %collective-permute-done.11.recv_ref = bf16[136,512]{1,0:T(8,128)(2,1)S(1)} collective-permute-done((bf16[136,512]{1,0:T(8,128)(2,1)S(1)}, bf16[136,512]{1,0:T(8,128)(2,1)S(1)}, u32[]{:S(2)}, u32[]{:S(2)}) %collective-permute-start.11) | collective-permute-done | bytes 139296 | tf_op jit(solution)/shard_map/ppermute | solution.py:297
  54.0 2.8 %collective-permute-start.13 = (bf16[72,512]{1,0:T(8,128)(2,1)S(1)}, bf16[72,512]{1,0:T(8,128)(2,1)S(1)}, u32[]{:S(2)}, u32[]{:S(2)}) collective-permute-start(bf16[72,512]{1,0:T(8,128)(2,1)S(1)} %get-tuple-element.41), channel_id=1, source_target_pairs={{0,192},{1,33},{32,224},{33,1},{64,128},{65,97},{96,160},{97,65},{... | collective-permute-start | bytes 221192 | tf_op jit(solution)/shard_map/ppermute | solution.py:297
  56.8 2.8 %collective-permute-start.12 = (bf16[72,512]{1,0:T(8,128)(2,1)S(1)}, bf16[72,512]{1,0:T(8,128)(2,1)S(1)}, u32[]{:S(2)}, u32[]{:S(2)}) collective-permute-start(bf16[72,512]{1,0:T(8,128)(2,1)S(1)} %get-tuple-element.40), channel_id=1, source_target_pairs={{0,192},{1,33},{32,224},{33,1},{64,128},{65,97},{96,160},{97,65},{... | collective-permute-start | bytes 221192 | tf_op jit(solution)/shard_map/ppermute | solution.py:297
  59.7 2.8 %collective-permute-done.12.refs_2_ = bf16[72,512]{1,0:T(8,128)(2,1)S(1)} collective-permute-done((bf16[72,512]{1,0:T(8,128)(2,1)S(1)}, bf16[72,512]{1,0:T(8,128)(2,1)S(1)}, u32[]{:S(2)}, u32[]{:S(2)}) %collective-permute-start.12) | collective-permute-done | bytes 73760 | tf_op jit(solution)/shard_map/ppermute | solution.py:297
  62.5 0.7 %finish.1 = (f32[64,1024]{1,0:T(8,128)}, f32[1,1024]{1,0:T(1,128)}) custom-call(f32[72,512]{1,0:T(8,128)S(1)} %get-tuple-element.32.refs_0_, f32[72,512]{1,0:T(8,128)S(1)} %get-tuple-element.39.refs_1_, bf16[72,512]{1,0:T(8,128)(2,1)S(1)} %collective-permute-done.12.refs_2_, bf16[72,512]{1,0:T(8,128)(2,1)S(1)} %collective-permute-done.13.refs_3_), custom_call_target="tpu_custom_call" | custom-call | tf_op jit(solution)/shard_map/finish/pallas_call | solution.py:275
  (22 shorter events, 2.6 us)
Async XLA Ops:
  1.3 0.8 %copy-start.1 = (f32[1024,8]{0,1:T(8,128)S(1)}, f32[1024,8]{0,1:T(8,128)}, u32[]{:S(2)}) copy-start(f32[1024,8]{0,1:T(8,128)} %param.6) | copy-start | bytes 98308
  2.0 29.9 %copy-start = (bf16[2048,1024]{1,0:T(8,128)(2,1)S(1)}, bf16[2048,1024]{1,0:T(8,128)(2,1)}, u32[]{:S(2)}) copy-start(bf16[2048,1024]{1,0:T(8,128)(2,1)} %rows_ref.3) | copy-start | bytes 12582916
  11.8 5.3 %collective-permute-start = (f32[1,2048]{1,0:T(1,128)S(1)}, f32[1,2048]{1,0:T(1,128)S(1)}, u32[]{:S(2)}, u32[]{:S(2)}) collective-permute-start(f32[1,2048]{1,0:T(1,128)S(1)} %get-tuple-element.24.refs_0_), channel_id=1, source_target_pairs={{0,4},{2,6},{4,8},{6,10},{8,12},{10,14},{12,16},{14,18},{16,20},{1... | collective-permute-start | bytes 24584 | tf_op jit(solution)/shard_map/ppermute | solution.py:287
  13.8 3.7 %collective-permute-start.1 = (f32[1,2048]{1,0:T(1,128)S(1)}, f32[1,2048]{1,0:T(1,128)S(1)}, u32[]{:S(2)}, u32[]{:S(2)}) collective-permute-start(f32[1,2048]{1,0:T(1,128)S(1)} %get-tuple-element.24.refs_0_), channel_id=1, source_target_pairs={{0,28},{2,30},{4,0},{6,2},{8,4},{10,6},{12,8},{14,10},{16,12},{18,... | collective-permute-start | bytes 24584 | tf_op jit(solution)/shard_map/ppermute | solution.py:287
  13.9 5.2 %collective-permute-start.2 = (f32[1,2048]{1,0:T(1,128)S(1)}, f32[1,2048]{1,0:T(1,128)S(1)}, u32[]{:S(2)}, u32[]{:S(2)}) collective-permute-start(f32[1,2048]{1,0:T(1,128)S(1)} %get-tuple-element.24.refs_0_), channel_id=1, source_target_pairs={{0,2},{2,0},{4,6},{6,4},{8,10},{10,8},{12,14},{14,12},{16,18},{18,... | collective-permute-start | bytes 24584 | tf_op jit(solution)/shard_map/ppermute | solution.py:287
  19.1 14.2 %collective-permute-start.3 = (f32[1,2048]{1,0:T(1,128)S(1)}, f32[1,2048]{1,0:T(1,128)S(1)}, u32[]{:S(2)}, u32[]{:S(2)}) collective-permute-start(f32[1,2048]{1,0:T(1,128)S(1)} %join.2.refs_0_), channel_id=1, source_target_pairs={{0,16},{2,18},{4,20},{6,22},{8,24},{10,26},{12,28},{14,30},{16,0},... | collective-permute-start | bytes 24584 | tf_op jit(solution)/shard_map/ppermute | solution.py:287
  25.4 8.2 %collective-permute-start.4 = (f32[1,2048]{1,0:T(1,128)S(1)}, f32[1,2048]{1,0:T(1,128)S(1)}, u32[]{:S(2)}, u32[]{:S(2)}) collective-permute-start(f32[1,2048]{1,0:T(1,128)S(1)} %join.2.refs_0_), channel_id=1, source_target_pairs={{0,10},{2,8},{4,14},{6,12},{8,18},{10,16},{12,22},{14,20},{16,26},... | collective-permute-start | bytes 24584 | tf_op jit(solution)/shard_map/ppermute | solution.py:287
  29.5 7.0 %collective-permute-start.5 = (f32[1,2048]{1,0:T(1,128)S(1)}, f32[1,2048]{1,0:T(1,128)S(1)}, u32[]{:S(2)}, u32[]{:S(2)}) collective-permute-start(f32[1,2048]{1,0:T(1,128)S(1)} %join.2.refs_0_), channel_id=1, source_target_pairs={{0,26},{2,24},{4,30},{6,28},{8,2},{10,0},{12,6},{14,4},{16,10},{18... | collective-permute-start | bytes 24584 | tf_op jit(solution)/shard_map/ppermute | solution.py:287
  38.9 3.1 %collective-permute-start.9 = (bf16[520,512]{1,0:T(8,128)(2,1)S(1)}, bf16[520,512]{1,0:T(8,128)(2,1)S(1)}, u32[]{:S(2)}, u32[]{:S(2)}) collective-permute-start(bf16[520,512]{1,0:T(8,128)(2,1)S(1)} %get-tuple-element.34), channel_id=1, source_target_pairs={{0,1},{1,0},{2,3},{3,2},{4,5},{5,4},{6,7},{7,6},{8,9},{9,8},{10,11... | collective-permute-start | bytes 1597448 | tf_op jit(solution)/shard_map/ppermute | solution.py:291
  41.5 2.1 %collective-permute-start.6 = (bf16[520,512]{1,0:T(8,128)(2,1)S(1)}, bf16[520,512]{1,0:T(8,128)(2,1)S(1)}, u32[]{:S(2)}, u32[]{:S(2)}) collective-permute-start(bf16[520,512]{1,0:T(8,128)(2,1)S(1)} %get-tuple-element.27), channel_id=1, source_target_pairs={{0,1},{1,0},{2,3},{3,2},{4,5},{5,4},{6,7},{7,6},{8,9},{9,8},{10,11... | collective-permute-start | bytes 1597448 | tf_op jit(solution)/shard_map/ppermute | solution.py:291
  42.2 6.5 %collective-permute-start.10 = (bf16[264,512]{1,0:T(8,128)(2,1)S(1)}, bf16[264,512]{1,0:T(8,128)(2,1)S(1)}, u32[]{:S(2)}, u32[]{:S(2)}) collective-permute-start(bf16[264,512]{1,0:T(8,128)(2,1)S(1)} %get-tuple-element.36), channel_id=1, source_target_pairs={{0,32},{1,65},{32,0},{33,97},{64,96},{65,1},{96,64},{97,33},{128,1... | collective-permute-start | bytes 811016 | tf_op jit(solution)/shard_map/ppermute | solution.py:297
  43.7 7.9 %collective-permute-start.7 = (bf16[264,512]{1,0:T(8,128)(2,1)S(1)}, bf16[264,512]{1,0:T(8,128)(2,1)S(1)}, u32[]{:S(2)}, u32[]{:S(2)}) collective-permute-start(bf16[264,512]{1,0:T(8,128)(2,1)S(1)} %get-tuple-element.29), channel_id=1, source_target_pairs={{0,32},{1,65},{32,0},{33,97},{64,96},{65,1},{96,64},{97,33},{128,1... | collective-permute-start | bytes 811016 | tf_op jit(solution)/shard_map/ppermute | solution.py:297
  48.8 5.1 %collective-permute-start.11 = (bf16[136,512]{1,0:T(8,128)(2,1)S(1)}, bf16[136,512]{1,0:T(8,128)(2,1)S(1)}, u32[]{:S(2)}, u32[]{:S(2)}) collective-permute-start(bf16[136,512]{1,0:T(8,128)(2,1)S(1)} %get-tuple-element.38), channel_id=1, source_target_pairs={{0,64},{1,193},{32,96},{33,225},{64,0},{65,129},{96,32},{97,161},{... | collective-permute-start | bytes 417800 | tf_op jit(solution)/shard_map/ppermute | solution.py:297
  51.7 5.1 %collective-permute-start.8 = (bf16[136,512]{1,0:T(8,128)(2,1)S(1)}, bf16[136,512]{1,0:T(8,128)(2,1)S(1)}, u32[]{:S(2)}, u32[]{:S(2)}) collective-permute-start(bf16[136,512]{1,0:T(8,128)(2,1)S(1)} %get-tuple-element.31), channel_id=1, source_target_pairs={{0,64},{1,193},{32,96},{33,225},{64,0},{65,129},{96,32},{97,161},{... | collective-permute-start | bytes 417800 | tf_op jit(solution)/shard_map/ppermute | solution.py:297
  54.0 5.7 %collective-permute-start.13 = (bf16[72,512]{1,0:T(8,128)(2,1)S(1)}, bf16[72,512]{1,0:T(8,128)(2,1)S(1)}, u32[]{:S(2)}, u32[]{:S(2)}) collective-permute-start(bf16[72,512]{1,0:T(8,128)(2,1)S(1)} %get-tuple-element.41), channel_id=1, source_target_pairs={{0,192},{1,33},{32,224},{33,1},{64,128},{65,97},{96,160},{97,65},{... | collective-permute-start | bytes 221192 | tf_op jit(solution)/shard_map/ppermute | solution.py:297
  56.8 5.7 %collective-permute-start.12 = (bf16[72,512]{1,0:T(8,128)(2,1)S(1)}, bf16[72,512]{1,0:T(8,128)(2,1)S(1)}, u32[]{:S(2)}, u32[]{:S(2)}) collective-permute-start(bf16[72,512]{1,0:T(8,128)(2,1)S(1)} %get-tuple-element.40), channel_id=1, source_target_pairs={{0,192},{1,33},{32,224},{33,1},{64,128},{65,97},{96,160},{97,65},{... | collective-permute-start | bytes 221192 | tf_op jit(solution)/shard_map/ppermute | solution.py:297
